TPU v7x, 512 devices: a whole 4x4x16 slice. The times are simulated.
512 devices in a mesh: dp: 8 (over z_lo), seq: 64 (over x, y, z_hi, core).
Axes of the slice: x: 4, y: 4, z: 16 (z_hi: 2, z_lo: 8; z = z_hi * 8 + z_lo), core: 2. Of those that a mesh axis runs over, the one named last changes fastest.
Arguments:
- queries: bfloat16 [65536, 2048], P(('dp', 'seq')), may hold values from -8 to 8
- keys: bfloat16 [65536, 1024], P(('dp', 'seq')), may hold values from -15 to 15
- values: bfloat16 [65536, 1024], P(('dp', 'seq')), may hold values from -6 to 6
- output_gradient: bfloat16 [65536, 2048], P(('dp', 'seq')), may hold values from -6 to 6
- doc_lengths: int32 [512], replicated, may hold values from 1 to 512, 65536 in all
Outputs:
- attended: bfloat16 [65536, 2048], P(('dp', 'seq'))
- q_grad: float32 [65536, 2048], P(('dp', 'seq'))
- k_grad: float32 [65536, 1024], P(('dp', 'seq'))
- v_grad: float32 [65536, 1024], P(('dp', 'seq'))
Inputs may be any that keep to these rules, and one draw needn't show every extreme that they name: `doc_lengths`: the documents fill all 65536 positions of the sequence in order, and the longest has exactly 512 tokens.
All inputs are finite; a program needn't handle non-finite values.
Results may differ from a plain program's by a relative error of at most 0.04.
Values may be sent and summed in bfloat16 or wider, within the bound.
A program may use at most 64 MiB of HBM per device.

v0:
```python
import jax
import jax.numpy as jnp
from jax import lax
from jax.sharding import PartitionSpec as P

QUERY_HEADS = 16
KEY_VALUE_HEADS = 8
HEAD_SIZE = 128
LOCAL_WINDOW = 256


score_scale = 168.0 ** (-0.5)


def passed_along(value, axis, steps):
    count = lax.axis_size(axis)
    leading, last = (max(0, -steps), min(count, count - steps))
    return lax.ppermute(value, axis, [(source, source + steps) for source in range(leading, last)])


def doc_index(positions, doc_ends):
    doc_count = jnp.sum((doc_ends[None, :] <= positions[:, None]).astype(jnp.int32), axis=1)
    return jnp.where(positions < 0, -1, doc_count)


def live_pairs(query_pos, key_pos, doc_ends):
    spacing = query_pos[:, None] - key_pos[None, :]
    same_doc = doc_index(query_pos, doc_ends)[:, None] == doc_index(key_pos, doc_ends)[None, :]
    return same_doc & (spacing >= 0) & (spacing < LOCAL_WINDOW)


def pair_scores(heads_of_queries, heads_of_keys, live_mask):
    raw_scores = jnp.einsum(
        "qgrd,kgd->grqk", heads_of_queries, heads_of_keys, preferred_element_type=jnp.float32
    )
    return jnp.where(live_mask[None, None], raw_scores * score_scale, -jnp.inf)


def weighted_values(scores, log_total, heads_of_values):
    weights = jnp.exp(scores - log_total[..., None]).astype(jnp.bfloat16)
    return jnp.einsum(
        "grqk,kgd->qgrd", weights, heads_of_values, preferred_element_type=jnp.float32
    )


def pair_grads(
    scores, log_total, grad_dot, heads_of_queries, head_gradients, heads_of_keys, heads_of_values
):
    probs_full = jnp.exp(scores - log_total[..., None])
    weights = probs_full.astype(jnp.bfloat16)
    prob_grad = jnp.einsum(
        "qgrd,kgd->grqk", head_gradients, heads_of_values, preferred_element_type=jnp.float32
    )
    score_grad = (probs_full * (prob_grad - grad_dot[..., None]) * score_scale).astype(jnp.bfloat16)
    query_part = jnp.einsum(
        "grqk,kgd->qgrd", score_grad, heads_of_keys, preferred_element_type=jnp.float32
    )
    key_portion = jnp.einsum(
        "grqk,qgrd->kgd", score_grad, heads_of_queries, preferred_element_type=jnp.float32
    )
    value_portion = jnp.einsum(
        "grqk,qgrd->kgd", weights, head_gradients, preferred_element_type=jnp.float32
    )
    return (query_part, key_portion, value_portion)


def on_device(queries, keys, values, output_gradient, doc_lengths):
    count_of_rows = queries.shape[0]
    query_groups = QUERY_HEADS // KEY_VALUE_HEADS
    halo_depth = max(1, LOCAL_WINDOW // count_of_rows)
    device_rank = lax.axis_index(("dp", "seq"))
    doc_ends = jnp.cumsum(doc_lengths)
    offsets = jnp.arange(count_of_rows, dtype=jnp.int32)
    query_pos = device_rank * count_of_rows + offsets
    heads_of_queries = queries.reshape(count_of_rows, KEY_VALUE_HEADS, query_groups, HEAD_SIZE)
    head_gradients = output_gradient.reshape(
        count_of_rows, KEY_VALUE_HEADS, query_groups, HEAD_SIZE
    )
    piece_list = [(keys, values)]
    for distance in range(1, halo_depth + 1):
        piece_list.append(passed_along((keys, values), ("dp", "seq"), distance))
    key_blocks = []
    for source_rows in range(halo_depth + 1):
        heads_of_keys = piece_list[source_rows][0].reshape(
            count_of_rows, KEY_VALUE_HEADS, HEAD_SIZE
        )
        heads_of_values = piece_list[source_rows][1].reshape(
            count_of_rows, KEY_VALUE_HEADS, HEAD_SIZE
        )
        live_mask = live_pairs(
            query_pos, (device_rank - source_rows) * count_of_rows + offsets, doc_ends
        )
        scores = pair_scores(heads_of_queries, heads_of_keys, live_mask)
        key_blocks.append((heads_of_keys, heads_of_values, live_mask, scores))
    row_max = jnp.max(key_blocks[0][3], axis=-1)
    for entry in key_blocks[1:]:
        row_max = jnp.maximum(row_max, jnp.max(entry[3], axis=-1))
    row_total = jnp.zeros_like(row_max)
    for entry in key_blocks:
        row_total = row_total + jnp.sum(jnp.exp(entry[3] - row_max[..., None]), axis=-1)
    log_total = row_max + jnp.log(row_total)
    context_rows = jnp.zeros((count_of_rows, KEY_VALUE_HEADS, query_groups, HEAD_SIZE), jnp.float32)
    for heads_of_keys, heads_of_values, live_mask, scores in key_blocks:
        context_rows = context_rows + weighted_values(scores, log_total, heads_of_values)
    attended = context_rows.reshape(count_of_rows, QUERY_HEADS * HEAD_SIZE).astype(jnp.bfloat16)
    output_widened = attended.astype(jnp.float32).reshape(
        count_of_rows, KEY_VALUE_HEADS, query_groups, HEAD_SIZE
    )
    grad_dot = jnp.transpose(
        jnp.sum(head_gradients.astype(jnp.float32) * output_widened, axis=-1), (1, 2, 0)
    )
    query_gradient = jnp.zeros(
        (count_of_rows, KEY_VALUE_HEADS, query_groups, HEAD_SIZE), jnp.float32
    )
    key_gradient = jnp.zeros((count_of_rows, KEY_VALUE_HEADS, HEAD_SIZE), jnp.float32)
    value_gradient = jnp.zeros((count_of_rows, KEY_VALUE_HEADS, HEAD_SIZE), jnp.float32)
    for source_rows in range(halo_depth + 1):
        heads_of_keys, heads_of_values, live_mask, scores = key_blocks[source_rows]
        if source_rows == 0:
            parts = pair_grads(
                scores,
                log_total,
                grad_dot,
                heads_of_queries,
                head_gradients,
                heads_of_keys,
                heads_of_values,
            )
            key_gradient = parts[1]
            value_gradient = parts[2]
        else:
            parts = pair_grads(
                scores,
                log_total,
                grad_dot,
                heads_of_queries,
                head_gradients,
                heads_of_keys,
                heads_of_values,
            )
            returned = (
                passed_along(parts[1].astype(jnp.bfloat16), ("dp", "seq"), -source_rows).astype(
                    jnp.float32
                ),
                passed_along(parts[2].astype(jnp.bfloat16), ("dp", "seq"), -source_rows).astype(
                    jnp.float32
                ),
            )
            key_gradient = key_gradient + returned[0]
            value_gradient = value_gradient + returned[1]
        query_gradient = query_gradient + parts[0]
    return (
        attended,
        query_gradient.reshape(count_of_rows, QUERY_HEADS * HEAD_SIZE),
        key_gradient.reshape(count_of_rows, KEY_VALUE_HEADS * HEAD_SIZE),
        value_gradient.reshape(count_of_rows, KEY_VALUE_HEADS * HEAD_SIZE),
    )


def solution(mesh):
    placed = (
        P(("dp", "seq"), None),
        P(("dp", "seq"), None),
        P(("dp", "seq"), None),
        P(("dp", "seq"), None),
        P(),
    )
    return jax.shard_map(
        on_device,
        mesh=mesh,
        in_specs=placed,
        out_specs=(
            P(("dp", "seq"), None),
            P(("dp", "seq"), None),
            P(("dp", "seq"), None),
            P(("dp", "seq"), None),
        ),
        check_vma=False,
    )
```

profile of v0, /device:TPU:40, one launch (start us, length us, event | category | flops | bytes accessed | tf_op | source)
XLA Modules:
  0.0 261.1 jit_solution(1019118782183938996)
XLA Ops:
  0.6 1.8 copy.89
  2.4 14.8 %collective-permute-start.1 = (bf16[128,1024]{0,1:T(8,128)(2,1)}, bf16[128,1024]{0,1:T(8,128)(2,1)S(1)}, u32[]{:S(2)}, u32[]{:S(2)}) collective-permute-start(bf16[128,1024]{0,1:T(8,128)(2,1)} %copy.89), channel_id=1, source_target_pairs={{0,2},{1,3},{2,4},{3,5},{4,6},{5,7},{6,8},{7,9},{8,10},{9,11},{10,... | collective-permute-start | bytes 786440 | tf_op jit(solution)/shard_map/ppermute | solution.py:18
  17.2 1.9 collective-permute-start
  19.2 1.9 collective-permute-start.3
  21.1 13.5 %collective-permute-start.2 = (bf16[128,1024]{1,0:T(8,128)(2,1)}, bf16[128,1024]{1,0:T(8,128)(2,1)}, u32[]{:S(2)}, u32[]{:S(2)}) collective-permute-start(bf16[128,1024]{1,0:T(8,128)(2,1)} %param.7), channel_id=1, source_target_pairs={{0,1},{1,2},{2,3},{3,4},{4,5},{5,6},{6,7},{7,8},{8,9},{9,10},{10,1... | collective-permute-start | bytes 786440 | tf_op jit(solution)/shard_map/ppermute | solution.py:18
  36.2 1.7 copy.178
  40.9 13.4 %collective-permute-done = bf16[128,1024]{0,1:T(8,128)(2,1)S(1)} collective-permute-done((bf16[128,1024]{0,1:T(8,128)(2,1)}, bf16[128,1024]{0,1:T(8,128)(2,1)S(1)}, u32[]{:S(2)}, u32[]{:S(2)}) %collective-permute-start) | collective-permute-done | bytes 262176 | tf_op jit(solution)/shard_map/ppermute | solution.py:18
  55.7 1.3 fusion.55
  58.0 1.3 fusion.30
  60.3 13.9 %collective-permute-done.2 = bf16[128,1024]{1,0:T(8,128)(2,1)} collective-permute-done((bf16[128,1024]{1,0:T(8,128)(2,1)}, bf16[128,1024]{1,0:T(8,128)(2,1)}, u32[]{:S(2)}, u32[]{:S(2)}) %collective-permute-start.2) | collective-permute-done | bytes 262176 | tf_op jit(solution)/shard_map/ppermute | solution.py:18
  74.3 1.8 copy.97
  76.0 2.6 convolution_add_fusion.3
  79.7 1.8 copy.99
  81.5 2.5 multiply_reduce_fusion
  86.8 12.3 %collective-permute-start.7 = (bf16[128,8,128]{0,2,1:T(8,128)(2,1)}, bf16[128,8,128]{0,2,1:T(8,128)(2,1)}, u32[]{:S(2)}, u32[]{:S(2)}) collective-permute-start(bf16[128,8,128]{0,2,1:T(8,128)(2,1)} %fusion.23), channel_id=1, source_target_pairs={{2,0},{3,1},{4,2},{5,3},{6,4},{7,5},{8,6},{9,7},{10,8},{11,9},{12,... | collective-permute-start | bytes 786440 | tf_op jit(solution)/shard_map/ppermute | solution.py:18
  99.2 128.6 %collective-permute-start.6 = (bf16[128,8,128]{0,2,1:T(8,128)(2,1)}, bf16[128,8,128]{0,2,1:T(8,128)(2,1)}, u32[]{:S(2)}, u32[]{:S(2)}) collective-permute-start(bf16[128,8,128]{0,2,1:T(8,128)(2,1)} %fusion.24), channel_id=1, source_target_pairs={{1,0},{2,1},{3,2},{4,3},{5,4},{6,5},{7,6},{8,7},{9,8},{10,9},{11,1... | collective-permute-start | bytes 786440 | tf_op jit(solution)/shard_map/ppermute | solution.py:18
  227.8 2.1 copy.123
  232.0 9.3 %collective-permute-start.4 = (bf16[128,8,128]{0,2,1:T(8,128)(2,1)}, bf16[128,8,128]{0,2,1:T(8,128)(2,1)}, u32[]{:S(2)}, u32[]{:S(2)}) collective-permute-start(bf16[128,8,128]{0,2,1:T(8,128)(2,1)} %fusion.26), channel_id=1, source_target_pairs={{1,0},{2,1},{3,2},{4,3},{5,4},{6,5},{7,6},{8,7},{9,8},{10,9},{11,1... | collective-permute-start | bytes 786440 | tf_op jit(solution)/shard_map/ppermute | solution.py:18
  241.4 2.0 collective-permute-start.5
  244.6 1.3 convolution_add_fusion
  245.9 2.5 copy.124
  248.4 1.3 convert_add_fusion
  250.8 7.9 %collective-permute-done.5 = bf16[128,8,128]{0,2,1:T(8,128)(2,1)} collective-permute-done((bf16[128,8,128]{0,2,1:T(8,128)(2,1)}, bf16[128,8,128]{0,2,1:T(8,128)(2,1)}, u32[]{:S(2)}, u32[]{:S(2)}) %collective-permute-start.5) | collective-permute-done | bytes 262176 | tf_op jit(solution)/shard_map/ppermute | solution.py:18
  258.7 1.4 convert_add_fusion.1
  (69 shorter events, 17.1 us)
Async XLA Ops:
  2.4 52.6 %collective-permute-start.1 = (bf16[128,1024]{0,1:T(8,128)(2,1)}, bf16[128,1024]{0,1:T(8,128)(2,1)S(1)}, u32[]{:S(2)}, u32[]{:S(2)}) collective-permute-start(bf16[128,1024]{0,1:T(8,128)(2,1)} %copy.89), channel_id=1, source_target_pairs={{0,2},{1,3},{2,4},{3,5},{4,6},{5,7},{6,8},{7,9},{8,10},{9,11},{10,... | collective-permute-start | bytes 786440 | tf_op jit(solution)/shard_map/ppermute | solution.py:18
  17.2 37.0 %collective-permute-start = (bf16[128,1024]{0,1:T(8,128)(2,1)}, bf16[128,1024]{0,1:T(8,128)(2,1)S(1)}, u32[]{:S(2)}, u32[]{:S(2)}) collective-permute-start(bf16[128,1024]{0,1:T(8,128)(2,1)} %copy.89), channel_id=1, source_target_pairs={{0,1},{1,2},{2,3},{3,4},{4,5},{5,6},{6,7},{7,8},{8,9},{9,10},{10,1... | collective-permute-start | bytes 786440 | tf_op jit(solution)/shard_map/ppermute | solution.py:18
  19.2 60.5 %collective-permute-start.3 = (bf16[128,1024]{1,0:T(8,128)(2,1)}, bf16[128,1024]{1,0:T(8,128)(2,1)}, u32[]{:S(2)}, u32[]{:S(2)}) collective-permute-start(bf16[128,1024]{1,0:T(8,128)(2,1)} %param.7), channel_id=1, source_target_pairs={{0,2},{1,3},{2,4},{3,5},{4,6},{5,7},{6,8},{7,9},{8,10},{9,11},{10,... | collective-permute-start | bytes 786440 | tf_op jit(solution)/shard_map/ppermute | solution.py:18
  21.1 53.2 %collective-permute-start.2 = (bf16[128,1024]{1,0:T(8,128)(2,1)}, bf16[128,1024]{1,0:T(8,128)(2,1)}, u32[]{:S(2)}, u32[]{:S(2)}) collective-permute-start(bf16[128,1024]{1,0:T(8,128)(2,1)} %param.7), channel_id=1, source_target_pairs={{0,1},{1,2},{2,3},{3,4},{4,5},{5,6},{6,7},{7,8},{8,9},{9,10},{10,1... | collective-permute-start | bytes 786440 | tf_op jit(solution)/shard_map/ppermute | solution.py:18
  34.6 0.7 copy-start.15
  36.2 1.8 copy-start.8
  37.9 1.0 copy-start.13
  39.0 1.0 copy-start.14
  40.8 16.9 %copy-start = (f32[8,2,128,128]{2,3,1,0:T(8,128)}, f32[8,2,128,128]{2,3,1,0:T(8,128)S(1)}, u32[]{:S(2)}) copy-start(f32[8,2,128,128]{2,3,1,0:T(8,128)S(1)} %get-tuple-element.28) | copy-start | bytes 3145732
  54.3 0.7 copy-start.11
  55.0 0.7 copy-start.9
  57.0 1.0 copy-start.4
  81.5 2.5 copy-start.6
  84.0 1.2 copy-start.7
  85.2 1.2 copy-start.1
  85.2 1.3 copy-start.5
  86.8 161.6 %collective-permute-start.7 = (bf16[128,8,128]{0,2,1:T(8,128)(2,1)}, bf16[128,8,128]{0,2,1:T(8,128)(2,1)}, u32[]{:S(2)}, u32[]{:S(2)}) collective-permute-start(bf16[128,8,128]{0,2,1:T(8,128)(2,1)} %fusion.23), channel_id=1, source_target_pairs={{2,0},{3,1},{4,2},{5,3},{6,4},{7,5},{8,6},{9,7},{10,8},{11,9},{12,... | collective-permute-start | bytes 786440 | tf_op jit(solution)/shard_map/ppermute | solution.py:18
  99.2 149.2 %collective-permute-start.6 = (bf16[128,8,128]{0,2,1:T(8,128)(2,1)}, bf16[128,8,128]{0,2,1:T(8,128)(2,1)}, u32[]{:S(2)}, u32[]{:S(2)}) collective-permute-start(bf16[128,8,128]{0,2,1:T(8,128)(2,1)} %fusion.24), channel_id=1, source_target_pairs={{1,0},{2,1},{3,2},{4,3},{5,4},{6,5},{7,6},{8,7},{9,8},{10,9},{11,1... | collective-permute-start | bytes 786440 | tf_op jit(solution)/shard_map/ppermute | solution.py:18
  227.8 2.1 copy-start.2
  229.9 1.1 copy-start.3
  232.0 11.6 %copy-start.12 = (bf16[128,1024]{0,1:T(8,128)(2,1)S(1)}, bf16[128,1024]{0,1:T(8,128)(2,1)}, u32[]{:S(2)}) copy-start(bf16[128,1024]{0,1:T(8,128)(2,1)} %copy-done.11) | copy-start | bytes 786436
  232.0 18.7 %collective-permute-start.4 = (bf16[128,8,128]{0,2,1:T(8,128)(2,1)}, bf16[128,8,128]{0,2,1:T(8,128)(2,1)}, u32[]{:S(2)}, u32[]{:S(2)}) collective-permute-start(bf16[128,8,128]{0,2,1:T(8,128)(2,1)} %fusion.26), channel_id=1, source_target_pairs={{1,0},{2,1},{3,2},{4,3},{5,4},{6,5},{7,6},{8,7},{9,8},{10,9},{11,1... | collective-permute-start | bytes 786440 | tf_op jit(solution)/shard_map/ppermute | solution.py:18
  241.4 17.3 %collective-permute-start.5 = (bf16[128,8,128]{0,2,1:T(8,128)(2,1)}, bf16[128,8,128]{0,2,1:T(8,128)(2,1)}, u32[]{:S(2)}, u32[]{:S(2)}) collective-permute-start(bf16[128,8,128]{0,2,1:T(8,128)(2,1)} %fusion.25), channel_id=1, source_target_pairs={{2,0},{3,1},{4,2},{5,3},{6,4},{7,5},{8,6},{9,7},{10,8},{11,9},{12,... | collective-permute-start | bytes 786440 | tf_op jit(solution)/shard_map/ppermute | solution.py:18
  243.7 1.0 copy-start.10
where the time goes:
time: 262 us; the launch traced here: 261 us
  starting transfers between devices  184 us (70%)
  waiting for transfers between devices  35.3 us (13%)
  matrix products  20 us (8%)
  local copies, waits for them, and re-layouts  19 us (7%)
    ppermute x8, starting transfers between devices, passed_along(): lax.ppermute(value, axis, [(source, source + steps) for source in range(l...  184 us
    ppermute x8, waiting for transfers between devices, passed_along(): lax.ppermute(value, axis, [(source, source + steps) for source in range(l...  35.3 us
    unnamed x40, local copies, waits for them, and re-layouts  14.6 us
    dot_general x3, matrix products, weighted_values(): jnp.einsum('grqk,kgd->qgrd', weights, heads_of_values, preferred_element_...  6.43 us
  transfers between devices with their start and end apart: 8, of which 3 were waited for; matrix products, arithmetic and copies ran while one was open for 10% of the time, Pallas kernels for 0%

commit v1 on v0

v1 whole, which is shorter than its diff:
```python
import jax
import jax.numpy as jnp
from jax import lax
from jax.experimental import pallas as pl
from jax.experimental.pallas import tpu as pltpu
from jax.sharding import PartitionSpec as P

HEAD = 128
ROWS = 128
CHIP_ROWS = 2 * ROWS
GROUPS = 4
QCOLS = 1024
KCOLS = 512
SCALE = 168.0 ** (-0.5)
MASKED = -1e30
MESH = pl.DeviceIdType.MESH
F32 = jnp.float32
BF16 = jnp.bfloat16


def dot_nn(a, b):
    return lax.dot_general(a, b, (((1,), (0,)), ((), ())), preferred_element_type=F32)


def dot_nt(a, b):
    return lax.dot_general(a, b, (((1,), (1,)), ((), ())), preferred_element_type=F32)


def dot_tn(a, b):
    return lax.dot_general(a, b, (((0,), (0,)), ((), ())), preferred_element_type=F32)


def make_kernel(dp_size, seq_size):
    chips = dp_size * seq_size // 2

    def place(chip, core):
        rank = chip * 2 + core
        return {"dp": rank // seq_size, "seq": lax.rem(rank, seq_size)}

    def kernel(
        q_ref, k_ref, v_ref, do_ref, len_ref,
        att_o, dq_o, dk_o, dv_o,
        qw, dow, kw, vw, halo, bias,
        att_st, dq_st, kv_full, kv_sib, ret_st, ret, out_st,
        in_l, in_s, in_r, halo_s, halo_r, ret_s, ret_r,
        res_l, res_s, res_r, fin,
    ):
        rank = lax.axis_index("dp") * seq_size + lax.axis_index("seq")
        chip = rank // 2
        core = lax.rem(rank, 2)
        other = 1 - core
        nxt = lax.rem(chip + 1, chips)
        prv = lax.rem(chip + chips - 1, chips)
        sibling = place(chip, other)
        mine = pl.multiple_of(core * ROWS, ROWS)
        theirs = pl.multiple_of(other * ROWS, ROWS)

        barrier = pltpu.get_barrier_semaphore()
        for peer in (sibling, place(nxt, 0), place(nxt, 1), place(prv, 0), place(prv, 1)):
            pl.semaphore_signal(barrier, inc=1, device_id=peer, device_id_type=MESH)

        operands = ((q_ref, qw, QCOLS), (do_ref, dow, QCOLS), (k_ref, kw, KCOLS), (v_ref, vw, KCOLS))

        def own_copy(i):
            src, dst, cols = operands[i]
            return pltpu.make_async_copy(
                src.at[:, pl.ds(pl.multiple_of(core * cols, cols), cols)],
                dst.at[pl.ds(mine, ROWS)], in_l.at[i])

        def sib_copy(i, rows):
            src, dst, cols = operands[i]
            return pltpu.make_async_remote_copy(
                src_ref=src.at[:, pl.ds(pl.multiple_of(other * cols, cols), cols)],
                dst_ref=dst.at[pl.ds(rows, ROWS)],
                send_sem=in_s.at[i], recv_sem=in_r.at[i],
                device_id=sibling, device_id_type=MESH)

        def halo_copy(g, dest, kv, rows, slot):
            src = (k_ref, v_ref)[kv]
            return pltpu.make_async_remote_copy(
                src_ref=src.at[:, pl.ds(pl.multiple_of(dest * KCOLS + g * HEAD, HEAD), HEAD)],
                dst_ref=halo.at[kv, g, pl.ds(rows, ROWS)],
                send_sem=halo_s.at[g, dest, kv], recv_sem=halo_r.at[g, slot, kv],
                device_id=place(nxt, dest), device_id_type=MESH)

        def ret_copy(g, dest, kv, slot):
            return pltpu.make_async_remote_copy(
                src_ref=ret_st.at[kv, g, pl.ds(dest * ROWS, ROWS)],
                dst_ref=ret.at[kv, slot, g],
                send_sem=ret_s.at[g, dest, kv], recv_sem=ret_r.at[g, slot, kv],
                device_id=place(prv, dest), device_id_type=MESH)

        def res_pairs(g, rows, half):
            cols = pl.multiple_of(half * QCOLS + g * 2 * HEAD, 2 * HEAD)
            return (
                (att_st.at[g, pl.ds(rows, ROWS)], att_o.at[:, pl.ds(cols, 2 * HEAD)]),
                (dq_st.at[g, pl.ds(rows, ROWS)], dq_o.at[:, pl.ds(cols, 2 * HEAD)]),
                (kv_full.at[0, g, pl.ds(rows, ROWS)], kv_sib.at[0, g]),
                (kv_full.at[1, g, pl.ds(rows, ROWS)], kv_sib.at[1, g]),
            )

        def res_remote(g, i, half):
            src, dst = res_pairs(g, theirs, half)[i]
            return pltpu.make_async_remote_copy(
                src_ref=src, dst_ref=dst, send_sem=res_s.at[g, i], recv_sem=res_r.at[g, i],
                device_id=sibling, device_id_type=MESH)

        def res_local(g, i):
            src, dst = res_pairs(g, mine, core)[i]
            return pltpu.make_async_copy(src, dst, res_l.at[g, i])

        for i in range(4):
            own_copy(i).start()
        pl.semaphore_wait(barrier, 5)

        def send_halo(g):
            for kv in range(2):
                for dest in range(2):
                    halo_copy(g, dest, kv, mine, core).start()

        send_halo(0)
        for i in range(4):
            sib_copy(i, mine).start()

        @pl.loop(1, GROUPS)
        def _(g):
            send_halo(g)

        lane = lax.broadcasted_iota(jnp.int32, (8, 512), 1)
        ends = jnp.broadcast_to(len_ref[...], (8, 512)).astype(F32)
        step = 1
        while step < 512:
            ends = ends + jnp.where(lane >= step, pltpu.roll(ends, step, 1), 0.0)
            step *= 2
        base = (chip * CHIP_ROWS).astype(F32)
        row = lax.broadcasted_iota(jnp.int32, (CHIP_ROWS, CHIP_ROWS), 0)
        col = lax.broadcasted_iota(jnp.int32, (CHIP_ROWS, CHIP_ROWS), 1)
        position = lax.broadcasted_iota(jnp.int32, (CHIP_ROWS, 512), 0).astype(F32) + base
        ends_b = jnp.broadcast_to(ends[0:1], (CHIP_ROWS, 512))
        first = jnp.max(jnp.where(ends_b <= position, ends_b, 0.0), axis=1, keepdims=True) - base
        own = col <= row
        key_pos = jnp.where(own, col, col - CHIP_ROWS).astype(F32)
        bias[...] = jnp.where(key_pos >= first, 0.0, MASKED)

        for i in range(4):
            own_copy(i).wait()
        for i in range(4):
            copy = sib_copy(i, theirs)
            copy.wait_send()
            copy.wait_recv()

        @pl.loop(0, GROUPS)
        def _(g):
            for slot in range(2):
                for kv in range(2):
                    halo_copy(g, 0, kv, slot * ROWS, slot).wait_recv()
            kcols = pl.ds(pl.multiple_of(g * HEAD, HEAD), HEAD)
            k_own = kw[:, kcols]
            v_own = vw[:, kcols]
            k_halo = halo[0, g]
            v_halo = halo[1, g]
            sums = None
            for r in range(2):
                qcols = pl.ds(pl.multiple_of(g * 2 * HEAD + r * HEAD, HEAD), HEAD)
                qh = qw[:, qcols]
                gh = dow[:, qcols]
                score = jnp.where(own, dot_nt(qh, k_own), dot_nt(qh, k_halo)) * SCALE + bias[...]
                top = jnp.max(score, axis=1, keepdims=True)
                e = jnp.exp(score - top)
                prob = e / jnp.sum(e, axis=1, keepdims=True)
                w_own = jnp.where(own, prob, 0.0).astype(BF16)
                w_halo = jnp.where(own, 0.0, prob).astype(BF16)
                att = (dot_nn(w_own, v_own) + dot_nn(w_halo, v_halo)).astype(BF16)
                att_st[g, :, r * HEAD:(r + 1) * HEAD] = att
                delta = jnp.sum(gh.astype(F32) * att.astype(F32), axis=1, keepdims=True)
                dprob = jnp.where(own, dot_nt(gh, v_own), dot_nt(gh, v_halo))
                ds = prob * (dprob - delta) * SCALE
                ds_own = jnp.where(own, ds, 0.0).astype(BF16)
                ds_halo = jnp.where(own, 0.0, ds).astype(BF16)
                dq_st[g, :, r * HEAD:(r + 1) * HEAD] = dot_nn(ds_own, k_own) + dot_nn(ds_halo, k_halo)
                part = (dot_tn(ds_halo, qh), dot_tn(w_halo, gh), dot_tn(ds_own, qh), dot_tn(w_own, gh))
                sums = part if sums is None else tuple(a + b for a, b in zip(sums, part))
            ret_st[0, g] = sums[0].astype(BF16)
            ret_st[1, g] = sums[1].astype(BF16)
            for kv in range(2):
                for dest in range(2):
                    ret_copy(g, dest, kv, core).start()
            kv_full[0, g] = sums[2]
            kv_full[1, g] = sums[3]
            for i in range(4):
                res_remote(g, i, core).start()
            for i in range(2):
                res_local(g, i).start()

        def fin_copy(g, half, kv):
            cols = pl.ds(pl.multiple_of(half * KCOLS + g * HEAD, HEAD), HEAD)
            return pltpu.make_async_copy(out_st.at[kv, half, g], (dk_o, dv_o)[kv].at[:, cols], fin.at[kv, half, g])

        @pl.loop(0, GROUPS)
        def _(g):
            for i in range(4):
                copy = res_remote(g, i, other)
                copy.wait_send()
                copy.wait_recv()
            for i in range(2):
                res_local(g, i).wait()
            for kv in range(2):
                for dest in range(2):
                    halo_copy(g, dest, kv, mine, core).wait_send()
                for slot in range(2):
                    ret_copy(g, slot, kv, slot).wait_recv()
                out_st[kv, core, g] = kv_full[kv, g, pl.ds(mine, ROWS)] + ret[kv, core, g].astype(F32)
                out_st[kv, other, g] = kv_sib[kv, g] + ret[kv, other, g].astype(F32)
                fin_copy(g, core, kv).start()
                fin_copy(g, other, kv).start()

        @pl.loop(0, GROUPS)
        def _(g):
            for kv in range(2):
                for dest in range(2):
                    ret_copy(g, dest, kv, core).wait_send()
                for half in range(2):
                    fin_copy(g, half, kv).wait()

    return kernel


def solution(mesh):
    dp_size, seq_size = mesh.shape["dp"], mesh.shape["seq"]
    kernel = make_kernel(dp_size, seq_size)
    anyspace = pl.BlockSpec(memory_space=pl.ANY)
    dma = pltpu.SemaphoreType.DMA

    def on_device(queries, keys, values, output_gradient, doc_lengths):
        return pl.pallas_call(
            kernel,
            out_shape=(
                jax.ShapeDtypeStruct((ROWS, 2048), BF16),
                jax.ShapeDtypeStruct((ROWS, 2048), F32),
                jax.ShapeDtypeStruct((ROWS, 1024), F32),
                jax.ShapeDtypeStruct((ROWS, 1024), F32),
            ),
            in_specs=[anyspace] * 4 + [pl.BlockSpec(memory_space=pltpu.VMEM)],
            out_specs=(anyspace,) * 4,
            scratch_shapes=[
                pltpu.VMEM((CHIP_ROWS, QCOLS), BF16),
                pltpu.VMEM((CHIP_ROWS, QCOLS), BF16),
                pltpu.VMEM((CHIP_ROWS, KCOLS), BF16),
                pltpu.VMEM((CHIP_ROWS, KCOLS), BF16),
                pltpu.VMEM((2, GROUPS, CHIP_ROWS, HEAD), BF16),
                pltpu.VMEM((CHIP_ROWS, CHIP_ROWS), F32),
                pltpu.VMEM((GROUPS, CHIP_ROWS, 2 * HEAD), BF16),
                pltpu.VMEM((GROUPS, CHIP_ROWS, 2 * HEAD), F32),
                pltpu.VMEM((2, GROUPS, CHIP_ROWS, HEAD), F32),
                pltpu.VMEM((2, GROUPS, ROWS, HEAD), F32),
                pltpu.VMEM((2, GROUPS, CHIP_ROWS, HEAD), BF16),
                pltpu.VMEM((2, 2, GROUPS, ROWS, HEAD), BF16),
                pltpu.VMEM((2, 2, GROUPS, ROWS, HEAD), F32),
                dma((4,)), dma((4,)), dma((4,)),
                dma((GROUPS, 2, 2)), dma((GROUPS, 2, 2)),
                dma((GROUPS, 2, 2)), dma((GROUPS, 2, 2)),
                dma((GROUPS, 2)), dma((GROUPS, 4)), dma((GROUPS, 4)),
                dma((2, 2, GROUPS)),
            ],
            compiler_params=pltpu.CompilerParams(
                collective_id=0, has_side_effects=True, vmem_limit_bytes=40 << 20),
        )(queries, keys, values, output_gradient, doc_lengths.reshape(1, -1))

    rows = P(("dp", "seq"), None)
    return jax.shard_map(
        on_device, mesh=mesh, in_specs=(rows,) * 4 + (P(),), out_specs=(rows,) * 4, check_vma=False)
```

time: 262 us -> 158 us (0.60)
  the two profiles are of different devices: /device:TPU:40 before, /device:TPU:33 now
where the time goes in v1:
time: 158 us
  Pallas kernels  149 us (94%)
  local copies, waits for them, and re-layouts  8.01 us (5%)
    pallas_call x1, Pallas kernels, on_device(): pl.pallas_call(kernel, out_shape=(jax.ShapeDtypeStruct((ROWS, 2048), BF16...  149 us
    unnamed x14, local copies, waits for them, and re-layouts  8.01 us

profile of v1, /device:TPU:33, one launch (start us, length us, event | category | flops | bytes accessed | tf_op | source)
XLA Modules:
  0.0 158.1 jit_solution(14770054628013407761)
XLA Ops:
  0.6 0.0 copy-start
  0.6 1.0 copy-done
  1.7 0.0 copy-start.1
  1.7 1.0 copy-done.1
  2.7 0.0 copy-start.2
  2.7 0.9 copy-done.2
  3.7 0.0 copy-start.3
  3.7 0.9 copy-done.3
  4.6 0.0 copy-start.4
  4.6 0.7 copy-done.4
  5.3 149.5 %shard_map.84 = (bf16[128,2048]{1,0:T(8,128)(2,1)S(1)}, f32[128,2048]{1,0:T(8,128)S(1)}, f32[128,1024]{1,0:T(8,128)S(1)}, f32[128,1024]{1,0:T(8,128)S(1)}) custom-call(bf16[128,2048]{1,0:T(8,128)(2,1)S(1)} %copy-done, bf16[128,1024]{1,0:T(8,128)(2,1)S(1)} %copy-done.2, bf16[128,1024]{1,0:T(8,128)(2,1)S(1)} %copy-done.3, bf16[128,2048]{1,0:T(8,128)(2,1)S(1)} %copy-done.1, ...), custom_call_target="tpu_custom_call" | custom-call | tf_op jit(solution)/shard_map/pallas_call | solution.py:235
  154.8 0.8 copy.13
  155.6 1.0 copy.14
  156.6 0.8 copy.15
  157.4 0.8 copy.16
Async XLA Ops:
  0.6 1.0 copy-start
  1.7 1.0 copy-start.1
  2.7 0.9 copy-start.2
  3.7 0.9 copy-start.3
  4.6 0.7 copy-start.4

commit v2 on v1

--- a/solution.py
+++ b/solution.py
@@ -13,6 +13,7 @@
 KCOLS = 512
 SCALE = 168.0 ** (-0.5)
 MASKED = -1e30
+VMEM_BYTES = 62 << 20
 MESH = pl.DeviceIdType.MESH
 F32 = jnp.float32
 BF16 = jnp.bfloat16
@@ -32,6 +33,7 @@
 
 def make_kernel(dp_size, seq_size):
     chips = dp_size * seq_size // 2
+    run = seq_size // 2
 
     def place(chip, core):
         rank = chip * 2 + core
@@ -42,8 +44,9 @@
         att_o, dq_o, dk_o, dv_o,
         qw, dow, kw, vw, halo, bias,
         att_st, dq_st, kv_full, kv_sib, ret_st, ret, out_st,
+        pass_h, pass_r,
         in_l, in_s, in_r, halo_s, halo_r, ret_s, ret_r,
-        res_l, res_s, res_r, fin,
+        res_l, res_s, res_r, fin, pass_hs, pass_hr, pass_rs, pass_rr,
     ):
         rank = lax.axis_index("dp") * seq_size + lax.axis_index("seq")
         chip = rank // 2
@@ -55,9 +58,56 @@
         mine = pl.multiple_of(core * ROWS, ROWS)
         theirs = pl.multiple_of(other * ROWS, ROWS)
 
+        line = chip // run
+        even = lax.rem(line, 2) == 0
+        src_wrap = lax.rem(chip, run) == run - 1
+        dst_wrap = lax.rem(chip, run) == 0
+        is_last = chip == chips - 1
+        is_first = chip == 0
+        sends_far = src_wrap & even
+        takes_far = dst_wrap & jnp.logical_not(even)
+        passes_h = dst_wrap & even
+        passes_r = src_wrap & jnp.logical_not(even)
+        sends_near = jnp.logical_not((src_wrap & even) | is_last)
+        takes_near = jnp.logical_not((dst_wrap & jnp.logical_not(even)) | is_first)
+        h_way = place(lax.rem(chip + chips - run + 1, chips), core)
+        r_way = place(lax.rem(chip + run - 1, chips), core)
+        h_from, h_to = lax.rem(chip + run - 1, chips), lax.rem(chip + run, chips)
+        r_from, r_to = lax.rem(chip + chips - run + 1, chips), lax.rem(chip + chips - run, chips)
+
         barrier = pltpu.get_barrier_semaphore()
-        for peer in (sibling, place(nxt, 0), place(nxt, 1), place(prv, 0), place(prv, 1)):
-            pl.semaphore_signal(barrier, inc=1, device_id=peer, device_id_type=MESH)
+
+        def greet(*peers):
+            for peer in peers:
+                pl.semaphore_signal(barrier, inc=1, device_id=peer, device_id_type=MESH)
+
+        greet(sibling)
+
+        @pl.when(sends_near)
+        def _():
+            greet(place(nxt, 0), place(nxt, 1))
+
+        @pl.when(takes_near)
+        def _():
+            greet(place(prv, 0), place(prv, 1))
+
+        @pl.when(passes_h)
+        def _():
+            greet(place(h_from, core), place(h_to, 0), place(h_to, 1))
+
+        @pl.when(passes_r)
+        def _():
+            greet(place(r_from, core), place(r_to, 0), place(r_to, 1))
+
+        @pl.when(sends_far)
+        def _():
+            back = lax.rem(chip + run, chips)
+            greet(h_way, place(back, 0), place(back, 1))
+
+        @pl.when(takes_far)
+        def _():
+            ahead = lax.rem(chip + chips - run, chips)
+            greet(r_way, place(ahead, 0), place(ahead, 1))
 
         operands = ((q_ref, qw, QCOLS), (do_ref, dow, QCOLS), (k_ref, kw, KCOLS), (v_ref, vw, KCOLS))
 
@@ -75,10 +125,12 @@
                 send_sem=in_s.at[i], recv_sem=in_r.at[i],
                 device_id=sibling, device_id_type=MESH)
 
+        def halo_src(g, dest, kv):
+            return (k_ref, v_ref)[kv].at[:, pl.ds(pl.multiple_of(dest * KCOLS + g * HEAD, HEAD), HEAD)]
+
         def halo_copy(g, dest, kv, rows, slot):
-            src = (k_ref, v_ref)[kv]
-            return pltpu.make_async_remote_copy(
-                src_ref=src.at[:, pl.ds(pl.multiple_of(dest * KCOLS + g * HEAD, HEAD), HEAD)],
+            return pltpu.make_async_remote_copy(
+                src_ref=halo_src(g, dest, kv),
                 dst_ref=halo.at[kv, g, pl.ds(rows, ROWS)],
                 send_sem=halo_s.at[g, dest, kv], recv_sem=halo_r.at[g, slot, kv],
                 device_id=place(nxt, dest), device_id_type=MESH)
@@ -111,12 +163,65 @@
 
         for i in range(4):
             own_copy(i).start()
-        pl.semaphore_wait(barrier, 5)
+
+        @pl.when(is_first)
+        def _():
+            halo[...] = jnp.zeros_like(halo)
+
+        @pl.when(is_last)
+        def _():
+            ret[...] = jnp.zeros_like(ret)
+
+        def far_copy(g, dest, kv):
+            return pltpu.make_async_remote_copy(
+                src_ref=halo_src(g, dest, kv), dst_ref=pass_h.at[g, dest, kv],
+                send_sem=halo_s.at[g, dest, kv], recv_sem=pass_hr.at[g, dest, kv],
+                device_id=h_way, device_id_type=MESH)
+
+        def far_ret(g, dest, kv):
+            return pltpu.make_async_remote_copy(
+                src_ref=ret_st.at[kv, g, pl.ds(dest * ROWS, ROWS)], dst_ref=pass_r.at[g, dest, kv],
+                send_sem=ret_s.at[g, dest, kv], recv_sem=pass_rr.at[g, dest, kv],
+                device_id=r_way, device_id_type=MESH)
+
+        def on_halo(g, dest, kv):
+            return pltpu.make_async_remote_copy(
+                src_ref=pass_h.at[g, dest, kv], dst_ref=halo.at[kv, g, pl.ds(mine, ROWS)],
+                send_sem=pass_hs.at[g, dest, kv], recv_sem=halo_r.at[g, core, kv],
+                device_id=place(h_to, dest), device_id_type=MESH)
+
+        def on_ret(g, dest, kv):
+            return pltpu.make_async_remote_copy(
+                src_ref=pass_r.at[g, dest, kv], dst_ref=ret.at[kv, core, g],
+                send_sem=pass_rs.at[g, dest, kv], recv_sem=ret_r.at[g, core, kv],
+                device_id=place(r_to, dest), device_id_type=MESH)
+
+        def far_arrival(buf, sem, g, dest, kv):
+            return pltpu.make_async_remote_copy(
+                src_ref=buf.at[g, dest, kv], dst_ref=buf.at[g, dest, kv],
+                send_sem=pass_hs.at[g, dest, kv], recv_sem=sem.at[g, dest, kv],
+                device_id=sibling, device_id_type=MESH)
+
+        pieces = [(dest, kv) for kv in range(2) for dest in range(2)]
+        zero = jnp.int32(0)
+        expected = (
+            1 + jnp.where(sends_near, 2, zero) + jnp.where(takes_near, 2, zero)
+            + jnp.where(passes_h, 3, zero) + jnp.where(passes_r, 3, zero)
+            + jnp.where(sends_far, 3, zero) + jnp.where(takes_far, 3, zero))
+        pl.semaphore_wait(barrier, expected)
 
         def send_halo(g):
-            for kv in range(2):
-                for dest in range(2):
-                    halo_copy(g, dest, kv, mine, core).start()
+            @pl.when(sends_near)
+            def _():
+                for kv in range(2):
+                    for dest in range(2):
+                        halo_copy(g, dest, kv, mine, core).start()
+
+            @pl.when(sends_far)
+            def _():
+                for kv in range(2):
+                    for dest in range(2):
+                        far_copy(g, dest, kv).start()
 
         send_halo(0)
         for i in range(4):
@@ -151,9 +256,18 @@
 
         @pl.loop(0, GROUPS)
         def _(g):
-            for slot in range(2):
-                for kv in range(2):
-                    halo_copy(g, 0, kv, slot * ROWS, slot).wait_recv()
+            @pl.when(passes_h)
+            def _():
+                for dest, kv in pieces:
+                    far_arrival(pass_h, pass_hr, g, dest, kv).wait_recv()
+                    on_halo(g, dest, kv).start()
+
+            @pl.when(jnp.logical_not(is_first))
+            def _():
+                for slot in range(2):
+                    for kv in range(2):
+                        halo_copy(g, 0, kv, slot * ROWS, slot).wait_recv()
+
             kcols = pl.ds(pl.multiple_of(g * HEAD, HEAD), HEAD)
             k_own = kw[:, kcols]
             v_own = vw[:, kcols]
@@ -182,9 +296,19 @@
                 sums = part if sums is None else tuple(a + b for a, b in zip(sums, part))
             ret_st[0, g] = sums[0].astype(BF16)
             ret_st[1, g] = sums[1].astype(BF16)
-            for kv in range(2):
-                for dest in range(2):
-                    ret_copy(g, dest, kv, core).start()
+
+            @pl.when(takes_near)
+            def _():
+                for kv in range(2):
+                    for dest in range(2):
+                        ret_copy(g, dest, kv, core).start()
+
+            @pl.when(takes_far)
+            def _():
+                for kv in range(2):
+                    for dest in range(2):
+                        far_ret(g, dest, kv).start()
+
             kv_full[0, g] = sums[2]
             kv_full[1, g] = sums[3]
             for i in range(4):
@@ -198,17 +322,28 @@
 
         @pl.loop(0, GROUPS)
         def _(g):
+            @pl.when(passes_r)
+            def _():
+                for dest, kv in pieces:
+                    far_arrival(pass_r, pass_rr, g, dest, kv).wait_recv()
+                    on_ret(g, dest, kv).start()
+
             for i in range(4):
                 copy = res_remote(g, i, other)
                 copy.wait_send()
                 copy.wait_recv()
             for i in range(2):
                 res_local(g, i).wait()
+
+            @pl.when(jnp.logical_not(is_last))
+            def _():
+                for kv in range(2):
+                    for dest in range(2):
+                        halo_copy(g, dest, kv, mine, core).wait_send()
+                    for slot in range(2):
+                        ret_copy(g, slot, kv, slot).wait_recv()
+
             for kv in range(2):
-                for dest in range(2):
-                    halo_copy(g, dest, kv, mine, core).wait_send()
-                for slot in range(2):
-                    ret_copy(g, slot, kv, slot).wait_recv()
                 out_st[kv, core, g] = kv_full[kv, g, pl.ds(mine, ROWS)] + ret[kv, core, g].astype(F32)
                 out_st[kv, other, g] = kv_sib[kv, g] + ret[kv, other, g].astype(F32)
                 fin_copy(g, core, kv).start()
@@ -216,11 +351,29 @@
 
         @pl.loop(0, GROUPS)
         def _(g):
+            @pl.when(jnp.logical_not(is_first))
+            def _():
+                for kv in range(2):
+                    for dest in range(2):
+                        ret_copy(g, dest, kv, core).wait_send()
+
             for kv in range(2):
-                for dest in range(2):
-                    ret_copy(g, dest, kv, core).wait_send()
                 for half in range(2):
                     fin_copy(g, half, kv).wait()
+
+        @pl.when(passes_h)
+        def _():
+            @pl.loop(0, GROUPS)
+            def _(g):
+                for dest, kv in pieces:
+                    on_halo(g, dest, kv).wait_send()
+
+        @pl.when(passes_r)
+        def _():
+            @pl.loop(0, GROUPS)
+            def _(g):
+                for dest, kv in pieces:
+                    on_ret(g, dest, kv).wait_send()
 
     return kernel
 
@@ -229,6 +382,7 @@
     dp_size, seq_size = mesh.shape["dp"], mesh.shape["seq"]
     kernel = make_kernel(dp_size, seq_size)
     anyspace = pl.BlockSpec(memory_space=pl.ANY)
+    in_hbm = pl.BlockSpec(memory_space=pltpu.HBM)
     dma = pltpu.SemaphoreType.DMA
 
     def on_device(queries, keys, values, output_gradient, doc_lengths):
@@ -240,7 +394,7 @@
                 jax.ShapeDtypeStruct((ROWS, 1024), F32),
                 jax.ShapeDtypeStruct((ROWS, 1024), F32),
             ),
-            in_specs=[anyspace] * 4 + [pl.BlockSpec(memory_space=pltpu.VMEM)],
+            in_specs=[in_hbm] * 4 + [pl.BlockSpec(memory_space=pltpu.VMEM)],
             out_specs=(anyspace,) * 4,
             scratch_shapes=[
                 pltpu.VMEM((CHIP_ROWS, QCOLS), BF16),
@@ -256,14 +410,17 @@
                 pltpu.VMEM((2, GROUPS, CHIP_ROWS, HEAD), BF16),
                 pltpu.VMEM((2, 2, GROUPS, ROWS, HEAD), BF16),
                 pltpu.VMEM((2, 2, GROUPS, ROWS, HEAD), F32),
+                pltpu.VMEM((GROUPS, 2, 2, ROWS, HEAD), BF16),
+                pltpu.VMEM((GROUPS, 2, 2, ROWS, HEAD), BF16),
                 dma((4,)), dma((4,)), dma((4,)),
                 dma((GROUPS, 2, 2)), dma((GROUPS, 2, 2)),
                 dma((GROUPS, 2, 2)), dma((GROUPS, 2, 2)),
                 dma((GROUPS, 2)), dma((GROUPS, 4)), dma((GROUPS, 4)),
                 dma((2, 2, GROUPS)),
+                dma((GROUPS, 2, 2)), dma((GROUPS, 2, 2)), dma((GROUPS, 2, 2)), dma((GROUPS, 2, 2)),
             ],
             compiler_params=pltpu.CompilerParams(
-                collective_id=0, has_side_effects=True, vmem_limit_bytes=40 << 20),
+                collective_id=0, has_side_effects=True, vmem_limit_bytes=VMEM_BYTES),
         )(queries, keys, values, output_gradient, doc_lengths.reshape(1, -1))
 
     rows = P(("dp", "seq"), None)

time: 158 us -> 135 us (0.85)
  the two profiles are of different devices: /device:TPU:33 before, /device:TPU:287 now
where the time goes in v2:
time: 135 us
  Pallas kernels  129 us (96%)
  local copies, waits for them, and re-layouts  5.39 us (4%)
    pallas_call x1, Pallas kernels, on_device(): pl.pallas_call(kernel, out_shape=(jax.ShapeDtypeStruct((ROWS, 2048), BF16...  129 us
    unnamed x10, local copies, waits for them, and re-layouts  5.39 us

profile of v2, /device:TPU:287, one launch (start us, length us, event | category | flops | bytes accessed | tf_op | source)
XLA Modules:
  0.0 134.6 jit_solution(13886679954010586398)
XLA Ops:
  0.6 128.6 %shard_map.84 = (bf16[128,2048]{1,0:T(8,128)(2,1)}, f32[128,2048]{1,0:T(8,128)}, f32[128,1024]{1,0:T(8,128)}, f32[128,1024]{1,0:T(8,128)}) custom-call(bf16[128,2048]{1,0:T(8,128)(2,1)} %q_ref.1, bf16[128,1024]{1,0:T(8,128)(2,1)} %k_ref.1, bf16[128,1024]{1,0:T(8,128)(2,1)} %v_ref.1, bf16[128,2048]{1,0:T(8,128)(2,1)} %do_ref.1, s32[1,512]{1,0:T(1,128)} %bitcast.1), custom_call_target="tpu_custom_call" | custom-call | tf_op jit(solution)/shard_map/pallas_call | solution.py:389
  129.2 0.0 copy-start
  129.2 2.0 %copy.13 = bf16[128,2048]{1,0:T(8,128)(2,1)} copy(bf16[128,2048]{1,0:T(8,128)(2,1)} %get-tuple-element.8) | data formatting | bytes 1048576
  131.2 0.0 copy-done
  131.2 0.0 copy-start.2
  131.2 1.0 copy.14
  132.2 0.4 copy-done.2
  132.6 0.0 copy-start.1
  132.6 0.8 copy.15
  133.4 0.4 copy-done.1
  133.8 0.8 copy.16
Async XLA Ops:
  129.2 2.0 %copy-start = (f32[128,2048]{1,0:T(8,128)S(1)}, f32[128,2048]{1,0:T(8,128)}, u32[]{:S(2)}) copy-start(f32[128,2048]{1,0:T(8,128)} %get-tuple-element.9) | copy-start | bytes 3145732
  131.2 1.4 %copy-start.2 = (f32[128,1024]{1,0:T(8,128)S(1)}, f32[128,1024]{1,0:T(8,128)}, u32[]{:S(2)}) copy-start(f32[128,1024]{1,0:T(8,128)} %get-tuple-element.10) | copy-start | bytes 1572868
  132.6 1.2 copy-start.1

commit v3 on v2

--- a/solution.py
+++ b/solution.py
@@ -13,6 +13,7 @@
 KCOLS = 512
 SCALE = 168.0 ** (-0.5)
 MASKED = -1e30
+FAR = 2
 VMEM_BYTES = 62 << 20
 MESH = pl.DeviceIdType.MESH
 F32 = jnp.float32
@@ -64,12 +65,12 @@
         dst_wrap = lax.rem(chip, run) == 0
         is_last = chip == chips - 1
         is_first = chip == 0
-        sends_far = src_wrap & even
-        takes_far = dst_wrap & jnp.logical_not(even)
-        passes_h = dst_wrap & even
-        passes_r = src_wrap & jnp.logical_not(even)
-        sends_near = jnp.logical_not((src_wrap & even) | is_last)
-        takes_near = jnp.logical_not((dst_wrap & jnp.logical_not(even)) | is_first)
+        sends_far = src_wrap & even & (line >= FAR)
+        takes_far = dst_wrap & jnp.logical_not(even) & (line >= FAR)
+        passes_h = dst_wrap & even & (line >= FAR)
+        passes_r = src_wrap & jnp.logical_not(even) & (line >= FAR)
+        sends_near = jnp.logical_not(sends_far | is_last)
+        takes_near = jnp.logical_not(takes_far | is_first)
         h_way = place(lax.rem(chip + chips - run + 1, chips), core)
         r_way = place(lax.rem(chip + run - 1, chips), core)
         h_from, h_to = lax.rem(chip + run - 1, chips), lax.rem(chip + run, chips)
@@ -316,18 +317,20 @@
             for i in range(2):
                 res_local(g, i).start()
 
+        @pl.when(passes_r)
+        def _():
+            @pl.loop(0, GROUPS)
+            def _(g):
+                for dest, kv in pieces:
+                    far_arrival(pass_r, pass_rr, g, dest, kv).wait_recv()
+                    on_ret(g, dest, kv).start()
+
         def fin_copy(g, half, kv):
             cols = pl.ds(pl.multiple_of(half * KCOLS + g * HEAD, HEAD), HEAD)
             return pltpu.make_async_copy(out_st.at[kv, half, g], (dk_o, dv_o)[kv].at[:, cols], fin.at[kv, half, g])
 
         @pl.loop(0, GROUPS)
         def _(g):
-            @pl.when(passes_r)
-            def _():
-                for dest, kv in pieces:
-                    far_arrival(pass_r, pass_rr, g, dest, kv).wait_recv()
-                    on_ret(g, dest, kv).start()
-
             for i in range(4):
                 copy = res_remote(g, i, other)
                 copy.wait_send()
@@ -378,6 +381,27 @@
     return kernel
 
 
+def hand_over(*refs):
+    sources, targets, holds, sem_in, sem_out = refs[:4], refs[4:8], refs[8:12], refs[12], refs[13]
+    parts = [(i, p) for p in range(4) for i in range(4)]
+
+    def take(i, p):
+        rows = pl.ds(p * (ROWS // 4), ROWS // 4)
+        return pltpu.make_async_copy(sources[i].at[rows], holds[i].at[rows], sem_in.at[i, p])
+
+    def give(i, p):
+        rows = pl.ds(p * (ROWS // 4), ROWS // 4)
+        return pltpu.make_async_copy(holds[i].at[rows], targets[i].at[rows], sem_out.at[i, p])
+
+    for part in parts:
+        take(*part).start()
+    for part in parts:
+        take(*part).wait()
+        give(*part).start()
+    for part in parts:
+        give(*part).wait()
+
+
 def solution(mesh):
     dp_size, seq_size = mesh.shape["dp"], mesh.shape["seq"]
     kernel = make_kernel(dp_size, seq_size)
@@ -386,14 +410,15 @@
     dma = pltpu.SemaphoreType.DMA
 
     def on_device(queries, keys, values, output_gradient, doc_lengths):
-        return pl.pallas_call(
+        results = (
+            jax.ShapeDtypeStruct((ROWS, 2048), BF16),
+            jax.ShapeDtypeStruct((ROWS, 2048), F32),
+            jax.ShapeDtypeStruct((ROWS, 1024), F32),
+            jax.ShapeDtypeStruct((ROWS, 1024), F32),
+        )
+        found = pl.pallas_call(
             kernel,
-            out_shape=(
-                jax.ShapeDtypeStruct((ROWS, 2048), BF16),
-                jax.ShapeDtypeStruct((ROWS, 2048), F32),
-                jax.ShapeDtypeStruct((ROWS, 1024), F32),
-                jax.ShapeDtypeStruct((ROWS, 1024), F32),
-            ),
+            out_shape=results,
             in_specs=[in_hbm] * 4 + [pl.BlockSpec(memory_space=pltpu.VMEM)],
             out_specs=(anyspace,) * 4,
             scratch_shapes=[
@@ -422,6 +447,14 @@
             compiler_params=pltpu.CompilerParams(
                 collective_id=0, has_side_effects=True, vmem_limit_bytes=VMEM_BYTES),
         )(queries, keys, values, output_gradient, doc_lengths.reshape(1, -1))
+        return pl.pallas_call(
+            hand_over,
+            out_shape=results,
+            in_specs=[in_hbm] * 4,
+            out_specs=(in_hbm,) * 4,
+            scratch_shapes=[pltpu.VMEM(r.shape, r.dtype) for r in results] + [dma((4, 4)), dma((4, 4))],
+            compiler_params=pltpu.CompilerParams(vmem_limit_bytes=VMEM_BYTES),
+        )(*found)
 
     rows = P(("dp", "seq"), None)
     return jax.shard_map(

time: 135 us -> 130 us (0.963)
  the two profiles are of different devices: /device:TPU:287 before, /device:TPU:351 now
where the time goes in v3:
time: 130 us
  Pallas kernels  129 us (99%)
    pallas_call x1, Pallas kernels, on_device(): pl.pallas_call(kernel, out_shape=results, in_specs=[in_hbm] * 4 + [pl.Blo...  127 us
    pallas_call x1, Pallas kernels, on_device(): pl.pallas_call(hand_over, out_shape=results, in_specs=[in_hbm] * 4, out_s...  2.74 us

profile of v3, /device:TPU:351, one launch (start us, length us, event | category | flops | bytes accessed | tf_op | source)
XLA Modules:
  0.0 129.9 jit_solution(15151658070871822539)
XLA Ops:
  0.6 126.5 %shard_map.84 = (bf16[128,2048]{1,0:T(8,128)(2,1)}, f32[128,2048]{1,0:T(8,128)}, f32[128,1024]{1,0:T(8,128)}, f32[128,1024]{1,0:T(8,128)}) custom-call(bf16[128,2048]{1,0:T(8,128)(2,1)} %q_ref.1, bf16[128,1024]{1,0:T(8,128)(2,1)} %k_ref.1, bf16[128,1024]{1,0:T(8,128)(2,1)} %v_ref.1, bf16[128,2048]{1,0:T(8,128)(2,1)} %do_ref.1, s32[1,512]{1,0:T(1,128)} %bitcast.1), custom_call_target="tpu_custom_call" | custom-call | tf_op jit(solution)/shard_map/pallas_call | solution.py:419
  127.2 2.7 %shard_map.85 = (bf16[128,2048]{1,0:T(8,128)(2,1)}, f32[128,2048]{1,0:T(8,128)}, f32[128,1024]{1,0:T(8,128)}, f32[128,1024]{1,0:T(8,128)}) custom-call(bf16[128,2048]{1,0:T(8,128)(2,1)} %get-tuple-element.8.refs_0_, f32[128,2048]{1,0:T(8,128)} %get-tuple-element.9.refs_1_, f32[128,1024]{1,0:T(8,128)} %get-tuple-element.10.refs_2_, ...), custom_call_target="tpu_custom_call" | custom-call | tf_op jit(solution)/shard_map/pallas_call | solution.py:450

commit v4 on v3

--- a/solution.py
+++ b/solution.py
@@ -14,6 +14,7 @@
 SCALE = 168.0 ** (-0.5)
 MASKED = -1e30
 FAR = 2
+FAR_BACK = 0
 VMEM_BYTES = 62 << 20
 MESH = pl.DeviceIdType.MESH
 F32 = jnp.float32
@@ -66,9 +67,11 @@
         is_last = chip == chips - 1
         is_first = chip == 0
         sends_far = src_wrap & even & (line >= FAR)
-        takes_far = dst_wrap & jnp.logical_not(even) & (line >= FAR)
+        takes_far = dst_wrap & jnp.logical_not(even) & (line >= FAR_BACK)
+        gets_far = dst_wrap & jnp.logical_not(even) & (line >= FAR)
+        owed_far = src_wrap & even & (line >= FAR_BACK)
         passes_h = dst_wrap & even & (line >= FAR)
-        passes_r = src_wrap & jnp.logical_not(even) & (line >= FAR)
+        passes_r = src_wrap & jnp.logical_not(even) & (line >= FAR_BACK)
         sends_near = jnp.logical_not(sends_far | is_last)
         takes_near = jnp.logical_not(takes_far | is_first)
         h_way = place(lax.rem(chip + chips - run + 1, chips), core)
@@ -84,11 +87,14 @@
 
         greet(sibling)
 
-        @pl.when(sends_near)
+        meets_nxt = jnp.logical_not(is_last | (sends_far & owed_far))
+        meets_prv = jnp.logical_not(is_first | (takes_far & gets_far))
+
+        @pl.when(meets_nxt)
         def _():
             greet(place(nxt, 0), place(nxt, 1))
 
-        @pl.when(takes_near)
+        @pl.when(meets_prv)
         def _():
             greet(place(prv, 0), place(prv, 1))
 
@@ -102,13 +108,21 @@
 
         @pl.when(sends_far)
         def _():
+            greet(h_way)
+
+        @pl.when(owed_far)
+        def _():
             back = lax.rem(chip + run, chips)
-            greet(h_way, place(back, 0), place(back, 1))
+            greet(place(back, 0), place(back, 1))
 
         @pl.when(takes_far)
         def _():
+            greet(r_way)
+
+        @pl.when(gets_far)
+        def _():
             ahead = lax.rem(chip + chips - run, chips)
-            greet(r_way, place(ahead, 0), place(ahead, 1))
+            greet(place(ahead, 0), place(ahead, 1))
 
         operands = ((q_ref, qw, QCOLS), (do_ref, dow, QCOLS), (k_ref, kw, KCOLS), (v_ref, vw, KCOLS))
 
@@ -205,10 +219,12 @@
 
         pieces = [(dest, kv) for kv in range(2) for dest in range(2)]
         zero = jnp.int32(0)
+        def some(count, cond):
+            return jnp.where(cond, count, zero)
+
         expected = (
-            1 + jnp.where(sends_near, 2, zero) + jnp.where(takes_near, 2, zero)
-            + jnp.where(passes_h, 3, zero) + jnp.where(passes_r, 3, zero)
-            + jnp.where(sends_far, 3, zero) + jnp.where(takes_far, 3, zero))
+            1 + some(2, meets_nxt) + some(2, meets_prv) + some(3, passes_h) + some(3, passes_r)
+            + some(1, sends_far) + some(2, owed_far) + some(1, takes_far) + some(2, gets_far))
         pl.semaphore_wait(barrier, expected)
 
         def send_halo(g):
@@ -257,11 +273,12 @@
 
         @pl.loop(0, GROUPS)
         def _(g):
-            @pl.when(passes_h)
-            def _():
-                for dest, kv in pieces:
-                    far_arrival(pass_h, pass_hr, g, dest, kv).wait_recv()
-                    on_halo(g, dest, kv).start()
+            @pl.when(passes_h & (g == 0))
+            def _():
+                for i in range(GROUPS):
+                    for dest, kv in pieces:
+                        far_arrival(pass_h, pass_hr, i, dest, kv).wait_recv()
+                        on_halo(i, dest, kv).start()
 
             @pl.when(jnp.logical_not(is_first))
             def _():

time: 130 us -> 128 us (0.985)
  the two profiles are of different devices: /device:TPU:351 before, /device:TPU:479 now
where the time goes in v4:
time: 128 us; the launch traced here: 127 us
  Pallas kernels  127 us (99%)
    pallas_call x1, Pallas kernels, on_device(): pl.pallas_call(kernel, out_shape=results, in_specs=[in_hbm] * 4 + [pl.Blo...  124 us
    pallas_call x1, Pallas kernels, on_device(): pl.pallas_call(hand_over, out_shape=results, in_specs=[in_hbm] * 4, out_s...  2.74 us

profile of v4, /device:TPU:479, one launch (start us, length us, event | category | flops | bytes accessed | tf_op | source)
XLA Modules:
  0.0 127.4 jit_solution(10682864369892825747)
XLA Ops:
  0.6 124.1 %shard_map.84 = (bf16[128,2048]{1,0:T(8,128)(2,1)}, f32[128,2048]{1,0:T(8,128)}, f32[128,1024]{1,0:T(8,128)}, f32[128,1024]{1,0:T(8,128)}) custom-call(bf16[128,2048]{1,0:T(8,128)(2,1)} %q_ref.1, bf16[128,1024]{1,0:T(8,128)(2,1)} %k_ref.1, bf16[128,1024]{1,0:T(8,128)(2,1)} %v_ref.1, bf16[128,2048]{1,0:T(8,128)(2,1)} %do_ref.1, s32[1,512]{1,0:T(1,128)} %bitcast.1), custom_call_target="tpu_custom_call" | custom-call | tf_op jit(solution)/shard_map/pallas_call | solution.py:436
  124.7 2.7 %shard_map.85 = (bf16[128,2048]{1,0:T(8,128)(2,1)}, f32[128,2048]{1,0:T(8,128)}, f32[128,1024]{1,0:T(8,128)}, f32[128,1024]{1,0:T(8,128)}) custom-call(bf16[128,2048]{1,0:T(8,128)(2,1)} %get-tuple-element.8.refs_0_, f32[128,2048]{1,0:T(8,128)} %get-tuple-element.9.refs_1_, f32[128,1024]{1,0:T(8,128)} %get-tuple-element.10.refs_2_, ...), custom_call_target="tpu_custom_call" | custom-call | tf_op jit(solution)/shard_map/pallas_call | solution.py:467

commit v5 on v4

--- a/solution.py
+++ b/solution.py
@@ -14,7 +14,7 @@
 SCALE = 168.0 ** (-0.5)
 MASKED = -1e30
 FAR = 2
-FAR_BACK = 0
+FAR_BACK = 2
 VMEM_BYTES = 62 << 20
 MESH = pl.DeviceIdType.MESH
 F32 = jnp.float32

time: 128 us -> 127 us (level)
  no operation moved by 1% of the time
where the time goes in v5:
time: 127 us
  Pallas kernels  126 us (99%)
    pallas_call x1, Pallas kernels, on_device(): pl.pallas_call(kernel, out_shape=results, in_specs=[in_hbm] * 4 + [pl.Blo...  123 us
    pallas_call x1, Pallas kernels, on_device(): pl.pallas_call(hand_over, out_shape=results, in_specs=[in_hbm] * 4, out_s...  2.74 us

profile of v5, /device:TPU:479, one launch (start us, length us, event | category | flops | bytes accessed | tf_op | source)
XLA Modules:
  0.0 126.5 jit_solution(2641444941643108940)
XLA Ops:
  0.6 123.1 %shard_map.84 = (bf16[128,2048]{1,0:T(8,128)(2,1)}, f32[128,2048]{1,0:T(8,128)}, f32[128,1024]{1,0:T(8,128)}, f32[128,1024]{1,0:T(8,128)}) custom-call(bf16[128,2048]{1,0:T(8,128)(2,1)} %q_ref.1, bf16[128,1024]{1,0:T(8,128)(2,1)} %k_ref.1, bf16[128,1024]{1,0:T(8,128)(2,1)} %v_ref.1, bf16[128,2048]{1,0:T(8,128)(2,1)} %do_ref.1, s32[1,512]{1,0:T(1,128)} %bitcast.1), custom_call_target="tpu_custom_call" | custom-call | tf_op jit(solution)/shard_map/pallas_call | solution.py:436
  123.8 2.7 %shard_map.85 = (bf16[128,2048]{1,0:T(8,128)(2,1)}, f32[128,2048]{1,0:T(8,128)}, f32[128,1024]{1,0:T(8,128)}, f32[128,1024]{1,0:T(8,128)}) custom-call(bf16[128,2048]{1,0:T(8,128)(2,1)} %get-tuple-element.8.refs_0_, f32[128,2048]{1,0:T(8,128)} %get-tuple-element.9.refs_1_, f32[128,1024]{1,0:T(8,128)} %get-tuple-element.10.refs_2_, ...), custom_call_target="tpu_custom_call" | custom-call | tf_op jit(solution)/shard_map/pallas_call | solution.py:467
